TPU v7x, 32 devices: a whole 2x2x4 slice. The times are simulated.
32 devices in a mesh: dp: 8 (over z, x), th: 2 (over core), tw: 2 (over y).
Axes of the slice: x: 2, y: 2, z: 4, core: 2. Of those that a mesh axis runs over, the one named last changes fastest.
Arguments:
- tokens: bfloat16 [16, 1536, 768], P('dp', ('th', 'tw')), may hold values from -6 to 6
- segment_ids: int32 [16, 1536], P('dp'), may hold values from 0 to 7, never falling along the last dimension, each value on 1 to 768 neighbouring positions
- norm1_gain: float32 [768], replicated, may hold values from 0.5 to 1.5
- norm1_shift: float32 [768], replicated, may hold values from -3 to 3
- w_qkv: bfloat16 [3, 768, 768], P(None, None, ('th', 'tw')), may hold values from -0.21875 to 0.21875
- b_qv: float32 [2, 768], P(None, ('th', 'tw')), may hold values from -3 to 3
- w_out: bfloat16 [768, 768], P(('th', 'tw')), may hold values from -0.875 to 0.875
- b_out: float32 [768], replicated, may hold values from -3 to 3
- norm2_gain: float32 [768], replicated, may hold values from 0.5 to 1.5
- norm2_shift: float32 [768], replicated, may hold values from -3 to 3
- w_up: bfloat16 [768, 3072], replicated, may hold values from -0.21875 to 0.21875
- b_up: float32 [3072], replicated, may hold values from -3 to 3
- w_down: bfloat16 [3072, 768], replicated, may hold values from -0.109375 to 0.109375
- b_down: float32 [768], replicated, may hold values from -3 to 3
- cotangent: bfloat16 [16, 1536, 768], P('dp', ('th', 'tw')), may hold values from -6 to 6
Outputs:
- block_out: bfloat16 [16, 1536, 768], P('dp', ('th', 'tw'))
- grad_tokens: bfloat16 [16, 1536, 768], P('dp', ('th', 'tw'))
- grad_norm1_gain: float32 [768], replicated
- grad_norm1_shift: float32 [768], replicated
- grad_w_qkv: float32 [3, 768, 768], P(None, None, ('th', 'tw'))
- grad_b_qv: float32 [2, 768], P(None, ('th', 'tw'))
- grad_w_out: float32 [768, 768], P(('th', 'tw'))
- grad_b_out: float32 [768], replicated
- grad_norm2_gain: float32 [768], replicated
- grad_norm2_shift: float32 [768], replicated
- grad_w_up: float32 [768, 3072], replicated
- grad_b_up: float32 [3072], replicated
- grad_w_down: float32 [3072, 768], replicated
- grad_b_down: float32 [768], replicated
Inputs may be any that keep to these rules, and one draw needn't show every extreme that they name: `segment_ids`: within each row the ids never fall, and one image holds 1 to 768 tokens.
All inputs are finite; a program needn't handle non-finite values.
Results may differ from a plain program's by a relative error of at most 0.015.
Values may be sent and summed in bfloat16 or wider, within the bound.
A program may use at most 192 MiB of HBM per device.

v0:
```python
import jax
import jax.numpy as jnp
from jax import lax
from jax.sharding import PartitionSpec as P

HD = 64
EPSILON = 1e-06


def layer_norm(field, norm_gain, norm_shift):
    average = jnp.mean(field, axis=-1, keepdims=True)
    centred = field - average
    spread = jnp.mean(centred * centred, axis=-1, keepdims=True)
    return centred * lax.rsqrt(spread + EPSILON) * norm_gain + norm_shift


def gelu_exact(field):
    return jax.nn.gelu(field, approximate=False)


def masked_scores(query_block, key_rows, row_seg, offset, block_rows):
    score_scale = query_block.shape[-1] ** (-0.5)
    same_image = row_seg[offset : offset + block_rows, None] == row_seg[None, :]
    scores = (
        jnp.einsum("qhe,khe->hqk", query_block, key_rows, preferred_element_type=jnp.float32)
        * score_scale
    )
    return jnp.where(same_image[None], scores, -1000000000.0)


def row_forward(row_items):
    row_qkv, row_seg = row_items
    length = row_qkv.shape[1]
    head_count = row_qkv.shape[2] // HD
    key_rows = row_qkv[1].reshape(length, head_count, HD)
    value_rows = row_qkv[2].reshape(length, head_count, HD)
    block_rows = min(512, length)
    head_outs = []
    log_totals = []
    for offset in range(0, length, block_rows):
        query_block = row_qkv[0, offset : offset + block_rows].reshape(block_rows, head_count, HD)
        scores = masked_scores(query_block, key_rows, row_seg, offset, block_rows)
        row_peak = jnp.max(scores, axis=-1, keepdims=True)
        exponent = jnp.exp(scores - row_peak)
        denominator = jnp.sum(exponent, axis=-1, keepdims=True)
        weights_low = (exponent / denominator).astype(jnp.bfloat16)
        head_out = jnp.einsum(
            "hqk,khe->qhe", weights_low, value_rows, preferred_element_type=jnp.float32
        )
        head_outs.append(head_out.reshape(block_rows, head_count * HD).astype(jnp.bfloat16))
        log_totals.append((row_peak + jnp.log(denominator))[..., 0])
    return (jnp.concatenate(head_outs, 0), jnp.concatenate(log_totals, 1))


def row_backward(row_items):
    row_qkv, row_grad, row_total, row_seg = row_items
    length = row_qkv.shape[1]
    head_count = row_qkv.shape[2] // HD
    score_scale = HD ** (-0.5)
    key_rows = row_qkv[1].reshape(length, head_count, HD)
    value_rows = row_qkv[2].reshape(length, head_count, HD)
    block_rows = min(512, length)
    key_grad = jnp.zeros((length, head_count, HD), jnp.float32)
    value_grad = jnp.zeros((length, head_count, HD), jnp.float32)
    query_grads = []
    for offset in range(0, length, block_rows):
        query_block = row_qkv[0, offset : offset + block_rows].reshape(block_rows, head_count, HD)
        upstream = row_grad[offset : offset + block_rows].reshape(block_rows, head_count, HD)
        scores = masked_scores(query_block, key_rows, row_seg, offset, block_rows)
        probability = jnp.exp(scores - row_total[:, offset : offset + block_rows, None])
        value_grad = value_grad + jnp.einsum(
            "hqk,qhe->khe",
            probability.astype(jnp.bfloat16),
            upstream,
            preferred_element_type=jnp.float32,
        )
        prob_grad = jnp.einsum(
            "qhe,khe->hqk", upstream, value_rows, preferred_element_type=jnp.float32
        )
        row_inner = jnp.sum(probability * prob_grad, axis=-1, keepdims=True)
        score_grad = (probability * (prob_grad - row_inner)).astype(jnp.bfloat16) * score_scale
        query_grad = jnp.einsum(
            "hqk,khe->qhe", score_grad, key_rows, preferred_element_type=jnp.float32
        )
        query_grads.append(query_grad.reshape(block_rows, head_count * HD))
        key_grad = key_grad + jnp.einsum(
            "hqk,qhe->khe", score_grad, query_block, preferred_element_type=jnp.float32
        )
    stacked = jnp.stack(
        [
            jnp.concatenate(query_grads, 0),
            key_grad.reshape(length, head_count * HD),
            value_grad.reshape(length, head_count * HD),
        ]
    )
    return stacked.astype(jnp.bfloat16)


def body(
    tokens,
    segment_ids,
    norm1_gain,
    norm1_shift,
    w_qkv,
    b_qv,
    w_out,
    b_out,
    norm2_gain,
    norm2_shift,
    w_up,
    b_up,
    w_down,
    b_down,
    cotangent,
):
    inputs = tokens.astype(jnp.float32)
    normed_one, norm_one_back = jax.vjp(layer_norm, inputs, norm1_gain, norm1_shift)
    normed_low = normed_one.astype(jnp.bfloat16)
    gathered = lax.all_gather(normed_low, ("th", "tw"), axis=1, tiled=True)
    bias_rows = jnp.stack([b_qv[0], jnp.zeros_like(b_qv[0]), b_qv[1]])
    projected = jnp.einsum("rld,cde->rcle", gathered, w_qkv, preferred_element_type=jnp.float32)
    projected_low = (projected + bias_rows[None, :, None, :]).astype(jnp.bfloat16)
    heads_out, totals = lax.map(row_forward, (projected_low, segment_ids))
    partial_out = jnp.einsum("rle,ed->rld", heads_out, w_out, preferred_element_type=jnp.float32)
    branch = (
        lax.psum_scatter(
            partial_out.astype(jnp.bfloat16), ("th", "tw"), scatter_dimension=1, tiled=True
        ).astype(jnp.float32)
        + b_out
    )
    middle = inputs + branch
    normed_two, norm_two_back = jax.vjp(layer_norm, middle, norm2_gain, norm2_shift)
    second_low = normed_two.astype(jnp.bfloat16)
    hidden_pre = (
        jnp.einsum("rld,df->rlf", second_low, w_up, preferred_element_type=jnp.float32) + b_up
    )
    activated, gelu_back = jax.vjp(gelu_exact, hidden_pre)
    active_low = activated.astype(jnp.bfloat16)
    block_out = middle + (
        jnp.einsum("rlf,fd->rld", active_low, w_down, preferred_element_type=jnp.float32) + b_down
    )
    upstream = cotangent.astype(jnp.float32)
    grad_w_down = jnp.einsum(
        "rlf,rld->fd", active_low, cotangent, preferred_element_type=jnp.float32
    )
    grad_b_down = jnp.sum(upstream, axis=(0, 1))
    grad_active = jnp.einsum("rld,fd->rlf", cotangent, w_down, preferred_element_type=jnp.float32)
    grad_hidden = gelu_back(grad_active)[0].astype(jnp.bfloat16)
    grad_w_up = jnp.einsum(
        "rld,rlf->df", second_low, grad_hidden, preferred_element_type=jnp.float32
    )
    grad_b_up = jnp.sum(grad_hidden.astype(jnp.float32), axis=(0, 1))
    grad_normed_two = jnp.einsum(
        "rlf,df->rld", grad_hidden, w_up, preferred_element_type=jnp.float32
    )
    grad_mid_norm, grad_gain_two, grad_shift_two = norm_two_back(grad_normed_two)
    grad_middle = upstream + grad_mid_norm
    grad_branch = grad_middle.astype(jnp.bfloat16)
    grad_b_out = jnp.sum(grad_branch.astype(jnp.float32), axis=(0, 1))
    grad_whole = lax.all_gather(grad_branch, ("th", "tw"), axis=1, tiled=True)
    grad_heads = jnp.einsum(
        "rld,ed->rle", grad_whole, w_out, preferred_element_type=jnp.float32
    ).astype(jnp.bfloat16)
    grad_w_out = jnp.einsum(
        "rle,rld->ed", heads_out, grad_whole, preferred_element_type=jnp.float32
    )
    grad_qkv = lax.map(row_backward, (projected_low, grad_heads, totals, segment_ids))
    grad_w_qkv = jnp.einsum("rld,rcle->cde", gathered, grad_qkv, preferred_element_type=jnp.float32)
    grad_b_qv = jnp.sum(grad_qkv[:, 0::2].astype(jnp.float32), axis=(0, 2))
    grad_normed = jnp.einsum("rcle,cde->rld", grad_qkv, w_qkv, preferred_element_type=jnp.float32)
    grad_tile = lax.psum_scatter(
        grad_normed.astype(jnp.bfloat16), ("th", "tw"), scatter_dimension=1, tiled=True
    ).astype(jnp.float32)
    grad_inputs, grad_gain_one, grad_shift_one = norm_one_back(grad_tile)
    grad_tokens = (grad_middle + grad_inputs).astype(jnp.bfloat16)
    head_sums = (
        lax.psum(grad_w_qkv.astype(jnp.bfloat16), "dp").astype(jnp.float32),
        lax.psum(grad_b_qv.astype(jnp.bfloat16), "dp").astype(jnp.float32),
        lax.psum(grad_w_out.astype(jnp.bfloat16), "dp").astype(jnp.float32),
    )
    shared = lax.psum(
        (
            grad_gain_one,
            grad_shift_one,
            grad_b_out,
            grad_gain_two,
            grad_shift_two,
            grad_w_up,
            grad_b_up,
            grad_w_down,
            grad_b_down,
        ),
        ("dp", "th", "tw"),
    )
    return (
        block_out.astype(jnp.bfloat16),
        grad_tokens,
        shared[0],
        shared[1],
        head_sums[0],
        head_sums[1],
        head_sums[2],
        shared[2],
        shared[3],
        shared[4],
        shared[5],
        shared[6],
        shared[7],
        shared[8],
    )


def solution(mesh):
    return jax.shard_map(
        body,
        mesh=mesh,
        in_specs=(
            P("dp", ("th", "tw"), None),
            P("dp", None),
            P(),
            P(),
            P(None, None, ("th", "tw")),
            P(None, ("th", "tw")),
            P(("th", "tw"), None),
            P(),
            P(),
            P(),
            P(),
            P(),
            P(),
            P(),
            P("dp", ("th", "tw"), None),
        ),
        out_specs=(
            P("dp", ("th", "tw"), None),
            P("dp", ("th", "tw"), None),
            P(),
            P(),
            P(None, None, ("th", "tw")),
            P(None, ("th", "tw")),
            P(("th", "tw"), None),
            P(),
            P(),
            P(),
            P(),
            P(),
            P(),
            P(),
        ),
        check_vma=False,
    )
```

profile of v0, /device:TPU:0, one launch (start us, length us, event | category | flops | bytes accessed | tf_op | source)
XLA Modules:
  0.0 1006.1 jit_solution(13144696597506998621)
XLA Ops:
  14.8 40.1 %all-gather.3.cloned.1.call-done = bf16[2,1536,768]{2,1,0:T(8,128)(2,1)} async-done(((bf16[2,384,768]{2,1,0:T(8,128)(2,1)}), bf16[2,1536,768]{2,1,0:T(8,128)(2,1)}) %all-gather.3.cloned.1.call-update) | async-done | bytes 4718608 | tf_op jit(solution)/shard_map/all_gather | solution.py:119
  54.9 6.7 fusion.154
  61.6 59.3 %while.22 = (s32[]{:T(128)}, bf16[2,1536,192]{1,2,0:T(8,128)(2,1)S(1)}, f32[2,3,1536]{2,1,0:T(4,128)S(1)}, bf16[2,3,1536,192]{2,3,1,0:T(8,128)(2,1)}, s32[2,1536...) while((s32[]{:T(128)}, bf16[2,1536,192]{1,2,0:T(8,128)(2,1)S(1)}, ...), condition=%wide.region_9.10_spmd, body=%wide.region_2.9_spmd.sunk | while | flops 1901302272 | bytes 107581632 | solution.py:123
  78.7 5.2 fusion.324
  87.4 3.5 fusion.325
  108.0 5.2 fusion.324
  120.9 4.9 convolution_convert_fusion
  125.9 47.9 %reduce-scatter.3.cloned.1.call-done = bf16[2,384,768]{2,1,0:T(8,128)(2,1)} async-done(((bf16[2,1536,768]{2,1,0:T(8,128)(2,1)}), bf16[2,384,768]{2,1,0:T(8,128)(2,1)}) %reduce-scatter.3.cloned.1.call-update) | async-done | bytes 1179664 | tf_op jit(solution)/shard_map/reduce_scatter | solution.py:126
  177.7 9.2 fusion.165
  186.9 23.4 %multiply_convert_fusion.3 = (bf16[2,384,3072]{2,1,0:T(8,128)(2,1)}, f32[2,384,3072]{2,1,0:T(8,128)}) fusion(f32[2,384,3072]{2,1,0:T(8,128)S(1)} %get-tuple-element.164, f32[3072]{0:T(1024)S(1)} %copy-done.45, u8[384,3072]{1,0:T(8,128)(4,1)S(1)} %get-tuple-element.78, u8[384,3072]{1,0:T(8,128)(4,1)S(1)} %get-tuple-element.77), kind=kLoop, calls=%fused_computation.126 | loop fusion | flops 167510016 | bytes 25964544 | tf_op jit(solution)/shard_map/convert_element_type | solution.py:138
  210.2 12.5 %convert_reduce_fusion = (f32[3072]{0:T(1024)}, bf16[2,384,3072]{2,1,0:T(8,128)(2,1)}) fusion(f32[2,384,3072]{2,1,0:T(8,128)} %get-tuple-element.123, bf16[2,384,768]{2,1,0:T(8,128)(2,1)S(1)} %copy-done.15, bf16[3072,768]{1,0:T(8,128)(2,1)} %param.31, f32[2,384,3072]{2,1,0:T(8,128)S(1)} %get-tuple-element.164, f32[3072]{0:T(1024)S(1)} %copy-done.45), kind=kOutput, calls=%fused_computation.124 | convolution fusion | flops 3663983616 | bytes 29515776 | tf_op jit(solution)/shard_map/rld,fd->rlf/dot_general | solution.py:147
  222.8 8.1 fusion.185
  235.7 37.6 %all-gather.5.cloned.1.call-done = bf16[2,1536,768]{2,1,0:T(8,128)(2,1)} async-done(((bf16[2,384,768]{2,1,0:T(8,128)(2,1)}), bf16[2,1536,768]{2,1,0:T(8,128)(2,1)}) %all-gather.5.cloned.1.call-update) | async-done | bytes 4718608 | tf_op jit(solution)/shard_map/all_gather | solution.py:160
  273.3 5.0 convolution_convert_fusion.1
  278.3 254.2 %while.23 = (s32[]{:T(128)}, bf16[2,3,1536,192]{2,3,1,0:T(8,128)(2,1)}, bf16[2,3,1536,192]{2,3,1,0:T(8,128)(2,1)}, s32[2,1536]{1,0:T(2,128)S(1)}, f32[2,3,1536]{...) while((s32[]{:T(128)}, ...), condition=%wide.region_19.20_spmd, body=%wide.region_15.19_spmd.sunk | while | flops 4682926080 | bytes 364640672 | solution.py:167
  294.2 4.3 copy-done.3
  300.4 5.2 fusion.371
  305.6 15.2 %fusion.377 = bf16[3,64,512]{2,1,0:T(8,128)(2,1)} fusion(bf16[1536,3,64]{0,2,1:T(8,128)(2,1)S(1)} %bitcast.312, f32[3,512,1536]{2,1,0:T(8,128)} %copy-done.4, f32[3,512,1536]{2,1,0:T(8,128)} %fusion.371), kind=kOutput, calls=%fused_computation.94.clone.1 | convolution fusion | flops 320965632 | bytes 19660800 | tf_op jit(solution)/shard_map/while/body/eval_jaxpr/hqk,khe->qhe/dot_general | solution.py:82
  320.8 15.3 %fusion.372 = f32[3,64,1536]{2,1,0:T(8,128)} fusion(bf16[512,3,64]{0,2,1:T(8,128)(2,1)} %bitcast.323, f32[3,512,1536]{2,1,0:T(8,128)} %copy-done.4, f32[3,512,1536]{2,1,0:T(8,128)} %fusion.371), kind=kOutput, calls=%fused_computation.63.clone.1 | convolution fusion | flops 320867328 | bytes 20250624 | tf_op jit(solution)/shard_map/while/body/eval_jaxpr/hqk,qhe->khe/dot_general | solution.py:86
  336.1 5.2 fusion.375
  341.3 14.4 %fusion.379 = bf16[3,64,512]{2,1,0:T(8,128)(2,1)S(1)} fusion(bf16[1536,3,64]{0,2,1:T(8,128)(2,1)S(1)} %bitcast.313, f32[3,512,1536]{2,1,0:T(8,128)} %copy-done.3, f32[3,512,1536]{2,1,0:T(8,128)} %fusion.375), kind=kOutput, calls=%fused_computation.92.clone.1 | convolution fusion | flops 320965632 | bytes 19660800 | tf_op jit(solution)/shard_map/while/body/eval_jaxpr/hqk,khe->qhe/dot_general | solution.py:82
  355.6 5.2 fusion.373
  360.8 15.0 %fusion.378 = bf16[3,64,512]{2,1,0:T(8,128)(2,1)} fusion(bf16[1536,3,64]{0,2,1:T(8,128)(2,1)S(1)} %bitcast.314, f32[3,512,1536]{2,1,0:T(8,128)} %copy-done.2, f32[3,512,1536]{2,1,0:T(8,128)} %fusion.373), kind=kOutput, calls=%fused_computation.93.clone.1 | convolution fusion | flops 320965632 | bytes 19660800 | tf_op jit(solution)/shard_map/while/body/eval_jaxpr/hqk,khe->qhe/dot_general | solution.py:82
  375.8 14.1 %fusion.374 = f32[3,64,1536]{2,1,0:T(8,128)} fusion(bf16[512,3,64]{0,2,1:T(8,128)(2,1)S(1)} %bitcast.321, f32[3,512,1536]{2,1,0:T(8,128)} %copy-done.2, f32[3,512,1536]{2,1,0:T(8,128)} %fusion.373), kind=kOutput, calls=%fused_computation.67.clone.1 | convolution fusion | flops 320867328 | bytes 20250624 | tf_op jit(solution)/shard_map/while/body/eval_jaxpr/hqk,qhe->khe/dot_general | solution.py:86
  389.9 14.1 %fusion.376 = bf16[3,64,1536]{2,1,0:T(8,128)(2,1)S(1)} fusion(f32[3,64,1536]{2,1,0:T(8,128)} %fusion.372, f32[3,64,1536]{2,1,0:T(8,128)} %fusion.374, bf16[512,3,64]{0,2,1:T(8,128)(2,1)S(1)} %bitcast.319, f32[3,512,1536]{2,1,0:T(8,128)} %copy-done.3, f32[3,512,1536]{2,1,0:T(8,128)} %fusion.375), kind=kOutput, calls=%fused_computation.79.clone.1 | convolution fusion | flops 321752064 | bytes 22020096 | tf_op jit(solution)/shard_map/while/body/eval_jaxpr/hqk,qhe->khe/dot_general | solution.py:86
  421.0 4.3 copy-done.3
  427.2 5.2 fusion.371
  432.4 15.2 %fusion.377 = bf16[3,64,512]{2,1,0:T(8,128)(2,1)} fusion(bf16[1536,3,64]{0,2,1:T(8,128)(2,1)S(1)} %bitcast.312, f32[3,512,1536]{2,1,0:T(8,128)} %copy-done.4, f32[3,512,1536]{2,1,0:T(8,128)} %fusion.371), kind=kOutput, calls=%fused_computation.94.clone.1 | convolution fusion | flops 320965632 | bytes 19660800 | tf_op jit(solution)/shard_map/while/body/eval_jaxpr/hqk,khe->qhe/dot_general | solution.py:82
  447.6 15.3 %fusion.372 = f32[3,64,1536]{2,1,0:T(8,128)} fusion(bf16[512,3,64]{0,2,1:T(8,128)(2,1)} %bitcast.323, f32[3,512,1536]{2,1,0:T(8,128)} %copy-done.4, f32[3,512,1536]{2,1,0:T(8,128)} %fusion.371), kind=kOutput, calls=%fused_computation.63.clone.1 | convolution fusion | flops 320867328 | bytes 20250624 | tf_op jit(solution)/shard_map/while/body/eval_jaxpr/hqk,qhe->khe/dot_general | solution.py:86
  462.9 5.2 fusion.375
  468.1 14.4 %fusion.379 = bf16[3,64,512]{2,1,0:T(8,128)(2,1)S(1)} fusion(bf16[1536,3,64]{0,2,1:T(8,128)(2,1)S(1)} %bitcast.313, f32[3,512,1536]{2,1,0:T(8,128)} %copy-done.3, f32[3,512,1536]{2,1,0:T(8,128)} %fusion.375), kind=kOutput, calls=%fused_computation.92.clone.1 | convolution fusion | flops 320965632 | bytes 19660800 | tf_op jit(solution)/shard_map/while/body/eval_jaxpr/hqk,khe->qhe/dot_general | solution.py:82
  482.5 5.2 fusion.373
  487.6 15.0 %fusion.378 = bf16[3,64,512]{2,1,0:T(8,128)(2,1)} fusion(bf16[1536,3,64]{0,2,1:T(8,128)(2,1)S(1)} %bitcast.314, f32[3,512,1536]{2,1,0:T(8,128)} %copy-done.2, f32[3,512,1536]{2,1,0:T(8,128)} %fusion.373), kind=kOutput, calls=%fused_computation.93.clone.1 | convolution fusion | flops 320965632 | bytes 19660800 | tf_op jit(solution)/shard_map/while/body/eval_jaxpr/hqk,khe->qhe/dot_general | solution.py:82
  502.6 14.1 %fusion.374 = f32[3,64,1536]{2,1,0:T(8,128)} fusion(bf16[512,3,64]{0,2,1:T(8,128)(2,1)S(1)} %bitcast.321, f32[3,512,1536]{2,1,0:T(8,128)} %copy-done.2, f32[3,512,1536]{2,1,0:T(8,128)} %fusion.373), kind=kOutput, calls=%fused_computation.67.clone.1 | convolution fusion | flops 320867328 | bytes 20250624 | tf_op jit(solution)/shard_map/while/body/eval_jaxpr/hqk,qhe->khe/dot_general | solution.py:86
  516.8 14.1 %fusion.376 = bf16[3,64,1536]{2,1,0:T(8,128)(2,1)S(1)} fusion(f32[3,64,1536]{2,1,0:T(8,128)} %fusion.372, f32[3,64,1536]{2,1,0:T(8,128)} %fusion.374, bf16[512,3,64]{0,2,1:T(8,128)(2,1)S(1)} %bitcast.319, f32[3,512,1536]{2,1,0:T(8,128)} %copy-done.3, f32[3,512,1536]{2,1,0:T(8,128)} %fusion.375), kind=kOutput, calls=%fused_computation.79.clone.1 | convolution fusion | flops 321752064 | bytes 22020096 | tf_op jit(solution)/shard_map/while/body/eval_jaxpr/hqk,qhe->khe/dot_general | solution.py:86
  532.5 4.6 fusion.177
  537.2 6.2 fusion.174
  543.4 7.7 bitcast_convert_fusion
  551.2 10.5 %convolution_bitcast_fusion = f32[3072,768]{1,0:T(8,128)} fusion(bf16[2,384,3072]{2,1,0:T(8,128)(2,1)} %get-tuple-element.122, bf16[2,384,768]{2,1,0:T(8,128)(2,1)} %param.33), kind=kOutput, calls=%fused_computation.140 | convolution fusion | flops 3623878656 | bytes 15335424 | tf_op jit(solution)/shard_map/rlf,rld->fd/dot_general | solution.py:143
  561.7 9.2 convolution_bitcast_fusion.1
  571.7 8.8 add_convert_fusion.3
  580.9 21.5 %psum.87 = bf16[2,192]{1,0:T(2,128)(2,1)S(1)} all-reduce(bf16[2,192]{1,0:T(2,128)(2,1)S(1)} %slice_reduce_fusion), channel_id=1, replica_groups=mesh['dp'=8,'th'=2,'tw'=2] {'dp'}, use_global_device_ids=true, to_apply=%region_29.30 | all-reduce | flops 384 | bytes 1536 | tf_op jit(solution)/shard_map/psum | solution.py:178
  603.0 20.8 %all-reduce.8.cloned.1.call-done = (bf16[3,768,192]{1,2,0:T(8,128)(2,1)}, bf16[192,768]{1,0:T(8,128)(2,1)}) async-done(((bf16[3,768,192]{1,2,0:T(8,128)(2,1)}, bf16[192,768]{1,0:T(8,128)(2,1)}), (bf16[3,768,192]{1,2,0:T(8,128)(2,1)}, bf16[192,768]{1,0:T(8,128)(2,1)})) %all-reduce.8.cloned.1.call-update) | async-done | bytes 1179664 | tf_op jit(solution)/shard_map/psum | solution.py:177
  628.1 45.2 %reduce-scatter.5.cloned.1.call-done = bf16[2,384,768]{2,1,0:T(8,128)(2,1)} async-done(((bf16[2,1536,768]{2,1,0:T(8,128)(2,1)}), bf16[2,384,768]{2,1,0:T(8,128)(2,1)}) %reduce-scatter.5.cloned.1.call-update) | async-done | bytes 1179664 | tf_op jit(solution)/shard_map/reduce_scatter | solution.py:171
  681.4 42.5 %all-reduce = (f32[768]{0:T(1024)}, f32[768]{0:T(1024)}, f32[768]{0:T(1024)}, f32[768]{0:T(1024)}, f32[768]{0:T(1024)}, /*index=5*/f32[3072]{0:T(1024)}, f32[768]{0:T(1024)}) all-reduce(f32[768]{0:T(1024)S(1)} %get-tuple-element.81, f32[768]{0:T(1024)S(1)} %get-tuple-element.85, ...), channel_id=1, replica_groups=mesh['dp'=8,'th'=2,'tw'=2] {'dp','th','tw'}, use_global_device_ids=true, to_apply=%region_24.25 | all-reduce | flops 7680 | bytes 61440 | tf_op jit(solution)/shard_map/psum | solution.py:181
  724.0 262.5 %all-reduce.6.cloned.1.call-done = (f32[768,3072]{1,0:T(8,128)}, f32[3072,768]{1,0:T(8,128)}) async-done(((f32[768,3072]{1,0:T(8,128)}, f32[3072,768]{1,0:T(8,128)}), (f32[768,3072]{1,0:T(8,128)}, f32[3072,768]{1,0:T(8,128)})) %all-reduce.6.cloned.1.call-update) | async-done | bytes 18874384 | tf_op jit(solution)/shard_map/psum | solution.py:181
  986.5 8.8 copy.59
  995.2 3.7 copy.60
  (228 shorter events, 112.1 us)
Async XLA Ops:
  7.2 47.7 %copy-start = (bf16[3,768,192]{1,2,0:T(8,128)(2,1)S(1)}, bf16[3,768,192]{1,2,0:T(8,128)(2,1)}, u32[]{:S(2)}) copy-start(bf16[3,768,192]{1,2,0:T(8,128)(2,1)} %param.23) | copy-start | bytes 2654212
  7.2 7.5 copy-start.48
  7.2 47.7 %all-gather.3.cloned.1.call-start = ((), (), s32[]{:S(2)}) async-start(), calls=%async_computation.2 | async-start | bytes 5898240 | tf_op jit(solution)/shard_map/all_gather | solution.py:119
  14.6 159.3 %reduce-scatter.3.cloned.1.call-start = ((), (), s32[]{:S(2)}) async-start(), calls=%async_computation.3 | async-start | bytes 5898240 | tf_op jit(solution)/shard_map/reduce_scatter | solution.py:126
  14.8 46.8 %copy-start.20 = (s32[2,1536]{1,0:T(2,128)S(1)}, s32[2,1536]{1,0:T(2,128)}, u32[]{:S(2)}) copy-start(s32[2,1536]{1,0:T(2,128)} %param.20) | copy-start | bytes 36868
  120.8 5.0 copy-start.17
  120.9 53.0 %copy-start.5 = (bf16[2,384,768]{2,1,0:T(8,128)(2,1)S(1)}, bf16[2,384,768]{2,1,0:T(8,128)(2,1)}, u32[]{:S(2)}) copy-start(bf16[2,384,768]{2,1,0:T(8,128)(2,1)} %param.19) | copy-start | bytes 3538948
  120.9 53.0 %copy-start.21 = (f32[768]{0:T(1024)S(1)}, f32[768]{0:T(1024)}, u32[]{:S(2)}) copy-start(f32[768]{0:T(1024)} %param.26) | copy-start | bytes 9220
  125.8 51.8 %copy-start.25 = (f32[768]{0:T(1024)S(1)}, f32[768]{0:T(1024)}, u32[]{:S(2)}) copy-start(f32[768]{0:T(1024)} %param.27) | copy-start | bytes 9220
  125.8 51.8 %copy-start.30 = (f32[768]{0:T(1024)S(1)}, f32[768]{0:T(1024)}, u32[]{:S(2)}) copy-start(f32[768]{0:T(1024)} %param.28) | copy-start | bytes 9220
  125.8 51.8 %copy-start.45 = (f32[3072]{0:T(1024)S(1)}, f32[3072]{0:T(1024)}, u32[]{:S(2)}) copy-start(f32[3072]{0:T(1024)} %param.30) | copy-start | bytes 36868
  125.8 147.5 %all-gather.5.cloned.1.call-start = ((), (), s32[]{:S(2)}) async-start(), calls=%async_computation.4 | async-start | bytes 5898240 | tf_op jit(solution)/shard_map/all_gather | solution.py:160
  175.7 57.2 %copy-start.23 = (f32[2,384]{1,0:T(2,128)}, f32[2,384]{1,0:T(2,128)S(1)}, u32[]{:S(2)}) copy-start(f32[2,384]{1,0:T(2,128)S(1)} %broadcast_multiply_fusion) | copy-start | bytes 9220
  177.7 55.3 %copy-start.27 = (f32[2,384]{1,0:T(2,128)}, f32[2,384]{1,0:T(2,128)S(1)}, u32[]{:S(2)}) copy-start(f32[2,384]{1,0:T(2,128)S(1)} %fusion.183) | copy-start | bytes 9220
  186.8 23.4 %copy-start.15 = (bf16[2,384,768]{2,1,0:T(8,128)(2,1)S(1)}, bf16[2,384,768]{2,1,0:T(8,128)(2,1)}, u32[]{:S(2)}) copy-start(bf16[2,384,768]{2,1,0:T(8,128)(2,1)} %param.33) | copy-start | bytes 3538948
  232.9 40.4 %copy-start.29 = (bf16[192,768]{1,0:T(8,128)(2,1)S(1)}, bf16[192,768]{1,0:T(8,128)(2,1)}, u32[]{:S(2)}) copy-start(bf16[192,768]{1,0:T(8,128)(2,1)} %param.25) | copy-start | bytes 884740
  232.9 45.4 %copy-start.39 = (f32[2,384]{1,0:T(2,128)}, f32[2,384]{1,0:T(2,128)S(1)}, u32[]{:S(2)}) copy-start(f32[2,384]{1,0:T(2,128)S(1)} %negate_multiply_fusion.2) | copy-start | bytes 9220
  235.7 388.1 %all-reduce.8.cloned.1.call-start = ((), (), s32[]{:S(2)}) async-start(), calls=%async_computation.7 | async-start | bytes 2359296 | tf_op jit(solution)/shard_map/psum | solution.py:177
  281.7 4.9 copy-start.12
  291.7 7.7 copy-start.4
  389.9 14.2 %copy-start.13 = (bf16[3,64,512]{2,1,0:T(8,128)(2,1)S(1)}, bf16[3,64,512]{2,1,0:T(8,128)(2,1)}, u32[]{:S(2)}) copy-start(bf16[3,64,512]{2,1,0:T(8,128)(2,1)} %fusion.377) | copy-start | bytes 589828 | tf_op jit(solution)/shard_map/while
  389.9 14.2 %copy-start.14 = (bf16[3,64,512]{2,1,0:T(8,128)(2,1)S(1)}, bf16[3,64,512]{2,1,0:T(8,128)(2,1)}, u32[]{:S(2)}) copy-start(bf16[3,64,512]{2,1,0:T(8,128)(2,1)} %fusion.378) | copy-start | bytes 589828 | tf_op jit(solution)/shard_map/while
  408.6 4.9 copy-start.12
  418.6 7.7 copy-start.4
  516.7 14.2 %copy-start.13 = (bf16[3,64,512]{2,1,0:T(8,128)(2,1)S(1)}, bf16[3,64,512]{2,1,0:T(8,128)(2,1)}, u32[]{:S(2)}) copy-start(bf16[3,64,512]{2,1,0:T(8,128)(2,1)} %fusion.377) | copy-start | bytes 589828 | tf_op jit(solution)/shard_map/while
  516.8 14.2 %copy-start.14 = (bf16[3,64,512]{2,1,0:T(8,128)(2,1)S(1)}, bf16[3,64,512]{2,1,0:T(8,128)(2,1)}, u32[]{:S(2)}) copy-start(bf16[3,64,512]{2,1,0:T(8,128)(2,1)} %fusion.378) | copy-start | bytes 589828 | tf_op jit(solution)/shard_map/while
  543.3 130.0 %reduce-scatter.5.cloned.1.call-start = ((), (), s32[]{:S(2)}) async-start(), calls=%async_computation.5 | async-start | bytes 5898240 | tf_op jit(solution)/shard_map/reduce_scatter | solution.py:171
  551.1 435.4 %all-reduce.6.cloned.1.call-start = ((), (), s32[]{:S(2)}) async-start(), calls=%async_computation.6 | async-start | bytes 37748736 | tf_op jit(solution)/shard_map/psum | solution.py:181
  551.1 10.6 %copy-start.6 = (bf16[2,384,768]{2,1,0:T(8,128)(2,1)S(1)}, bf16[2,384,768]{2,1,0:T(8,128)(2,1)}, u32[]{:S(2)}) copy-start(bf16[2,384,768]{2,1,0:T(8,128)(2,1)} %param.19) | copy-start | bytes 3538948
  551.1 10.6 %copy-start.8 = (bf16[2,384,768]{2,1,0:T(8,128)(2,1)S(1)}, bf16[2,384,768]{2,1,0:T(8,128)(2,1)}, u32[]{:S(2)}) copy-start(bf16[2,384,768]{2,1,0:T(8,128)(2,1)} %reduce-scatter.3.cloned.1.call-done) | copy-start | bytes 3538948
  551.2 10.5 %copy-start.22 = (f32[768]{0:T(1024)S(1)}, f32[768]{0:T(1024)}, u32[]{:S(2)}) copy-start(f32[768]{0:T(1024)} %param.26) | copy-start | bytes 9220
  551.2 10.5 %copy-start.24 = (f32[2,384]{1,0:T(2,128)S(1)}, f32[2,384]{1,0:T(2,128)}, u32[]{:S(2)}) copy-start(f32[2,384]{1,0:T(2,128)} %copy-done.23) | copy-start | bytes 9220
  551.2 10.5 %copy-start.26 = (f32[768]{0:T(1024)S(1)}, f32[768]{0:T(1024)}, u32[]{:S(2)}) copy-start(f32[768]{0:T(1024)} %param.27) | copy-start | bytes 9220
  551.2 10.5 %copy-start.28 = (f32[2,384]{1,0:T(2,128)S(1)}, f32[2,384]{1,0:T(2,128)}, u32[]{:S(2)}) copy-start(f32[2,384]{1,0:T(2,128)} %copy-done.27) | copy-start | bytes 9220
  551.2 10.5 %copy-start.31 = (f32[768]{0:T(1024)S(1)}, f32[768]{0:T(1024)}, u32[]{:S(2)}) copy-start(f32[768]{0:T(1024)} %param.28) | copy-start | bytes 9220
  571.7 8.8 copy-start.19
  580.5 92.9 %copy-start.33 = (f32[2,384]{1,0:T(2,128)S(1)}, f32[2,384]{1,0:T(2,128)}, u32[]{:S(2)}) copy-start(f32[2,384]{1,0:T(2,128)} %copy-done.32) | copy-start | bytes 9220
  580.5 92.9 %copy-start.34 = (f32[768]{0:T(1024)S(1)}, f32[768]{0:T(1024)}, u32[]{:S(2)}) copy-start(f32[768]{0:T(1024)} %param.21) | copy-start | bytes 9220
  580.5 95.1 %copy-start.42 = (f32[2,384]{1,0:T(2,128)S(1)}, f32[2,384]{1,0:T(2,128)}, u32[]{:S(2)}) copy-start(f32[2,384]{1,0:T(2,128)} %copy-done.41) | copy-start | bytes 9220
  580.5 95.1 %copy-start.38 = (f32[2,384]{1,0:T(2,128)S(1)}, f32[2,384]{1,0:T(2,128)}, u32[]{:S(2)}) copy-start(f32[2,384]{1,0:T(2,128)} %copy-done.37) | copy-start | bytes 9220
  580.9 97.5 %copy-start.36 = (f32[2,384]{1,0:T(2,128)S(1)}, f32[2,384]{1,0:T(2,128)}, u32[]{:S(2)}) copy-start(f32[2,384]{1,0:T(2,128)} %copy-done.35) | copy-start | bytes 9220
  580.9 97.5 %copy-start.40 = (f32[2,384]{1,0:T(2,128)S(1)}, f32[2,384]{1,0:T(2,128)}, u32[]{:S(2)}) copy-start(f32[2,384]{1,0:T(2,128)} %copy-done.39) | copy-start | bytes 9220
  673.3 5.1 copy-start.10
  673.3 5.1 copy-start.11
  673.3 5.1 copy-start.16
  986.5 8.8 slice-start
  986.5 8.8 slice-start.1
  986.5 8.8 slice-start.2
  (18 other events, 56.0 us)
Sparse Core Ops, SparseCore 0:
  14.7 40.1 all-gather.2
  126.0 47.8 reduce-scatter.2
  235.8 37.4 all-gather.4
  543.5 80.2 all-reduce.7
  626.2 47.1 reduce-scatter.4
  681.3 305.1 all-reduce.5
where the time goes:
time: 1010 us
  waiting for transfers between devices  454 us (45%)
  matrix products  354 us (35%)
  other arithmetic  75.9 us (8%)
  blocking collectives  64 us (6%)
  local copies, waits for them, and re-layouts  40.5 us (4%)
  between operations  14.8 us (1%)
    psum x1, waiting for transfers between devices, body(): lax.psum((grad_gain_one, grad_shift_one, grad_b_out, grad_gain_two, grad_...  263 us
    dot_general x6, matrix products, row_backward(): jnp.einsum('hqk,khe->qhe', score_grad, key_rows, preferred_element_type=j...  89.1 us
    dot_general x6, matrix products, row_backward(): jnp.einsum('hqk,qhe->khe', score_grad, query_block, preferred_element_typ...  87.3 us
    reduce_scatter x1, waiting for transfers between devices, body(): lax.psum_scatter(partial_out.astype(jnp.bfloat16), ('th', 'tw'), scatter_...  47.9 us
    reduce_scatter x1, waiting for transfers between devices, body(): lax.psum_scatter(grad_normed.astype(jnp.bfloat16), ('th', 'tw'), scatter_...  45.2 us
    psum x1, blocking collectives, body(): lax.psum((grad_gain_one, grad_shift_one, grad_b_out, grad_gain_two, grad_...  42.5 us
    all_gather x1, waiting for transfers between devices, body(): gathered = lax.all_gather(normed_low, ('th', 'tw'), axis=1, tiled=True)  40.1 us
    all_gather x1, waiting for transfers between devices, body(): grad_whole = lax.all_gather(grad_branch, ('th', 'tw'), axis=1, tiled=True)  37.6 us
  transfers between devices with their start and end apart: 6, of which 6 were waited for; matrix products, arithmetic and copies ran while one was open for 5% of the time, Pallas kernels for 0%

commit v1 on v0

--- a/solution.py
+++ b/solution.py
@@ -5,6 +5,7 @@
 
 HD = 64
 EPSILON = 1e-06
+sites_direct = lambda mat: jax.lax.all_gather(mat, "dp").sum(axis=0)
 
 
 def layer_norm(field, norm_gain, norm_shift):
@@ -174,7 +175,7 @@
     grad_inputs, grad_gain_one, grad_shift_one = norm_one_back(grad_tile)
     grad_tokens = (grad_middle + grad_inputs).astype(jnp.bfloat16)
     head_sums = (
-        lax.psum(grad_w_qkv.astype(jnp.bfloat16), "dp").astype(jnp.float32),
+        sites_direct(grad_w_qkv.astype(jnp.bfloat16)).astype(jnp.float32),
         lax.psum(grad_b_qv.astype(jnp.bfloat16), "dp").astype(jnp.float32),
         lax.psum(grad_w_out.astype(jnp.bfloat16), "dp").astype(jnp.float32),
     )

time: 1010 us -> 1100 us (1.089)
  waiting for transfers between devices: 454 us -> 544 us
    all_gather x0 -> x1, waiting for transfers between devices: none -> 61.8 us  [sites_direct = lambda mat: jax.lax.all_gather(mat, 'dp').sum(axis=0)]
    psum x1, waiting for transfers between devices: 263 us -> 305 us  [body(): lax.psum((grad_gain_one, grad_shift_one, grad_b_out, grad_gain_two, grad_...]
    psum x1, waiting for transfers between devices: 20.8 us -> 4.2 us  [body(): lax.psum(grad_w_out.astype(jnp.bfloat16), 'dp').astype(jnp.float32)]
  transfers between devices with their start and end apart: 6 -> 7, of which waited for: 6 -> 7; matrix products, arithmetic and copies ran while one was open for 5% -> 5% of each run, Pallas kernels for 0% -> 0%
where the time goes in v1:
time: 1100 us
  waiting for transfers between devices  544 us (49%)
  matrix products  356 us (32%)
  other arithmetic  79 us (7%)
  blocking collectives  64.1 us (6%)
  local copies, waits for them, and re-layouts  40.5 us (4%)
  between operations  14.8 us (1%)
    psum x1, waiting for transfers between devices, body(): lax.psum((grad_gain_one, grad_shift_one, grad_b_out, grad_gain_two, grad_...  305 us
    dot_general x6, matrix products, row_backward(): jnp.einsum('hqk,khe->qhe', score_grad, key_rows, preferred_element_type=j...  89.4 us
    dot_general x6, matrix products, row_backward(): jnp.einsum('hqk,qhe->khe', score_grad, query_block, preferred_element_typ...  87.3 us
    all_gather x1, waiting for transfers between devices, sites_direct = lambda mat: jax.lax.all_gather(mat, 'dp').sum(axis=0)  61.8 us
    reduce_scatter x1, waiting for transfers between devices, body(): lax.psum_scatter(partial_out.astype(jnp.bfloat16), ('th', 'tw'), scatter_...  47.9 us
    reduce_scatter x1, waiting for transfers between devices, body(): lax.psum_scatter(grad_normed.astype(jnp.bfloat16), ('th', 'tw'), scatter_...  47.5 us
    psum x1, blocking collectives, body(): lax.psum((grad_gain_one, grad_shift_one, grad_b_out, grad_gain_two, grad_...  42.8 us
    all_gather x1, waiting for transfers between devices, body(): gathered = lax.all_gather(normed_low, ('th', 'tw'), axis=1, tiled=True)  40.1 us
  transfers between devices with their start and end apart: 7, of which 7 were waited for; matrix products, arithmetic and copies ran while one was open for 5% of the time, Pallas kernels for 0%

profile of v1, /device:TPU:0, one launch (start us, length us, event | category | flops | bytes accessed | tf_op | source)
XLA Modules:
  0.0 1100.8 jit_solution(15991996567226168997)
XLA Ops:
  14.8 40.1 %all-gather.5.cloned.1.call-done = bf16[2,1536,768]{2,1,0:T(8,128)(2,1)} async-done(((bf16[2,384,768]{2,1,0:T(8,128)(2,1)}), bf16[2,1536,768]{2,1,0:T(8,128)(2,1)}) %all-gather.5.cloned.1.call-update) | async-done | bytes 4718608 | tf_op jit(solution)/shard_map/all_gather | solution.py:120
  54.9 6.8 fusion.154
  61.6 59.3 %while.22 = (s32[]{:T(128)}, bf16[2,1536,192]{1,2,0:T(8,128)(2,1)S(1)}, f32[2,3,1536]{2,1,0:T(4,128)S(1)}, bf16[2,3,1536,192]{2,3,1,0:T(8,128)(2,1)}, s32[2,1536...) while((s32[]{:T(128)}, bf16[2,1536,192]{1,2,0:T(8,128)(2,1)S(1)}, ...), condition=%wide.region_9.10_spmd, body=%wide.region_2.9_spmd.sunk | while | flops 1901302272 | bytes 107581632 | solution.py:124
  78.8 5.2 fusion.324
  108.0 5.2 fusion.324
  120.9 4.9 convolution_convert_fusion
  126.0 47.9 %reduce-scatter.3.cloned.1.call-done = bf16[2,384,768]{2,1,0:T(8,128)(2,1)} async-done(((bf16[2,1536,768]{2,1,0:T(8,128)(2,1)}), bf16[2,384,768]{2,1,0:T(8,128)(2,1)}) %reduce-scatter.3.cloned.1.call-update) | async-done | bytes 1179664 | tf_op jit(solution)/shard_map/reduce_scatter | solution.py:127
  177.7 9.2 fusion.165
  186.9 23.4 %multiply_convert_fusion.3 = (bf16[2,384,3072]{2,1,0:T(8,128)(2,1)}, f32[2,384,3072]{2,1,0:T(8,128)}) fusion(f32[2,384,3072]{2,1,0:T(8,128)S(1)} %get-tuple-element.162, f32[3072]{0:T(1024)S(1)} %copy-done.44, u8[384,3072]{1,0:T(8,128)(4,1)S(1)} %get-tuple-element.78, u8[384,3072]{1,0:T(8,128)(4,1)S(1)} %get-tuple-element.77), kind=kLoop, calls=%fused_computation.126 | loop fusion | flops 167510016 | bytes 25964544 | tf_op jit(solution)/shard_map/convert_element_type | solution.py:139
  210.3 12.5 %convert_reduce_fusion = (f32[3072]{0:T(1024)}, bf16[2,384,3072]{2,1,0:T(8,128)(2,1)}) fusion(f32[2,384,3072]{2,1,0:T(8,128)} %get-tuple-element.121, bf16[2,384,768]{2,1,0:T(8,128)(2,1)S(1)} %copy-done.15, bf16[3072,768]{1,0:T(8,128)(2,1)} %param.31, f32[2,384,3072]{2,1,0:T(8,128)S(1)} %get-tuple-element.162, f32[3072]{0:T(1024)S(1)} %copy-done.44), kind=kOutput, calls=%fused_computation.124 | convolution fusion | flops 3663983616 | bytes 29515776 | tf_op jit(solution)/shard_map/rld,fd->rlf/dot_general | solution.py:148
  222.8 8.1 fusion.185
  235.8 37.6 %all-gather.7.cloned.1.call-done = bf16[2,1536,768]{2,1,0:T(8,128)(2,1)} async-done(((bf16[2,384,768]{2,1,0:T(8,128)(2,1)}), bf16[2,1536,768]{2,1,0:T(8,128)(2,1)}) %all-gather.7.cloned.1.call-update) | async-done | bytes 4718608 | tf_op jit(solution)/shard_map/all_gather | solution.py:161
  273.4 5.0 convolution_convert_fusion.1
  278.4 254.5 %while.23 = (s32[]{:T(128)}, bf16[2,3,1536,192]{2,3,1,0:T(8,128)(2,1)}, bf16[2,3,1536,192]{2,3,1,0:T(8,128)(2,1)}, s32[2,1536]{1,0:T(2,128)S(1)}, f32[2,3,1536]{...) while((s32[]{:T(128)}, ...), condition=%wide.region_19.20_spmd, body=%wide.region_15.19_spmd.sunk | while | flops 4682926080 | bytes 364640672 | solution.py:168
  294.3 4.3 copy-done.3
  300.5 5.2 fusion.371
  305.6 15.2 %fusion.377 = bf16[3,64,512]{2,1,0:T(8,128)(2,1)} fusion(bf16[1536,3,64]{0,2,1:T(8,128)(2,1)S(1)} %bitcast.313, f32[3,512,1536]{2,1,0:T(8,128)} %copy-done.4, f32[3,512,1536]{2,1,0:T(8,128)} %fusion.371), kind=kOutput, calls=%fused_computation.94.clone.1 | convolution fusion | flops 320965632 | bytes 19660800 | tf_op jit(solution)/shard_map/while/body/eval_jaxpr/hqk,khe->qhe/dot_general | solution.py:83
  320.8 15.3 %fusion.372 = f32[3,64,1536]{2,1,0:T(8,128)} fusion(bf16[512,3,64]{0,2,1:T(8,128)(2,1)} %bitcast.325, f32[3,512,1536]{2,1,0:T(8,128)} %copy-done.4, f32[3,512,1536]{2,1,0:T(8,128)} %fusion.371), kind=kOutput, calls=%fused_computation.63.clone.1 | convolution fusion | flops 320867328 | bytes 20250624 | tf_op jit(solution)/shard_map/while/body/eval_jaxpr/hqk,qhe->khe/dot_general | solution.py:87
  336.2 5.2 fusion.375
  341.3 14.3 %fusion.379 = bf16[3,64,512]{2,1,0:T(8,128)(2,1)S(1)} fusion(bf16[1536,3,64]{0,2,1:T(8,128)(2,1)S(1)} %bitcast.314, f32[3,512,1536]{2,1,0:T(8,128)} %copy-done.3, f32[3,512,1536]{2,1,0:T(8,128)} %fusion.375), kind=kOutput, calls=%fused_computation.92.clone.1 | convolution fusion | flops 320965632 | bytes 19660800 | tf_op jit(solution)/shard_map/while/body/eval_jaxpr/hqk,khe->qhe/dot_general | solution.py:83
  355.7 5.2 fusion.373
  360.8 15.2 %fusion.378 = bf16[3,64,512]{2,1,0:T(8,128)(2,1)} fusion(bf16[1536,3,64]{0,2,1:T(8,128)(2,1)S(1)} %bitcast.315, f32[3,512,1536]{2,1,0:T(8,128)} %copy-done.2, f32[3,512,1536]{2,1,0:T(8,128)} %fusion.373), kind=kOutput, calls=%fused_computation.93.clone.1 | convolution fusion | flops 320965632 | bytes 19660800 | tf_op jit(solution)/shard_map/while/body/eval_jaxpr/hqk,khe->qhe/dot_general | solution.py:83
  376.0 14.3 %fusion.374 = f32[3,64,1536]{2,1,0:T(8,128)} fusion(bf16[512,3,64]{0,2,1:T(8,128)(2,1)S(1)} %bitcast.323, f32[3,512,1536]{2,1,0:T(8,128)} %copy-done.2, f32[3,512,1536]{2,1,0:T(8,128)} %fusion.373), kind=kOutput, calls=%fused_computation.67.clone.1 | convolution fusion | flops 320867328 | bytes 20250624 | tf_op jit(solution)/shard_map/while/body/eval_jaxpr/hqk,qhe->khe/dot_general | solution.py:87
  390.4 13.9 %fusion.376 = bf16[3,64,1536]{2,1,0:T(8,128)(2,1)S(1)} fusion(f32[3,64,1536]{2,1,0:T(8,128)} %fusion.372, f32[3,64,1536]{2,1,0:T(8,128)} %fusion.374, bf16[512,3,64]{0,2,1:T(8,128)(2,1)S(1)} %bitcast.321, f32[3,512,1536]{2,1,0:T(8,128)} %copy-done.3, f32[3,512,1536]{2,1,0:T(8,128)} %fusion.375), kind=kOutput, calls=%fused_computation.79.clone.1 | convolution fusion | flops 321752064 | bytes 22020096 | tf_op jit(solution)/shard_map/while/body/eval_jaxpr/hqk,qhe->khe/dot_general | solution.py:87
  421.3 4.3 copy-done.3
  427.5 5.2 fusion.371
  432.6 15.2 %fusion.377 = bf16[3,64,512]{2,1,0:T(8,128)(2,1)} fusion(bf16[1536,3,64]{0,2,1:T(8,128)(2,1)S(1)} %bitcast.313, f32[3,512,1536]{2,1,0:T(8,128)} %copy-done.4, f32[3,512,1536]{2,1,0:T(8,128)} %fusion.371), kind=kOutput, calls=%fused_computation.94.clone.1 | convolution fusion | flops 320965632 | bytes 19660800 | tf_op jit(solution)/shard_map/while/body/eval_jaxpr/hqk,khe->qhe/dot_general | solution.py:83
  447.8 15.3 %fusion.372 = f32[3,64,1536]{2,1,0:T(8,128)} fusion(bf16[512,3,64]{0,2,1:T(8,128)(2,1)} %bitcast.325, f32[3,512,1536]{2,1,0:T(8,128)} %copy-done.4, f32[3,512,1536]{2,1,0:T(8,128)} %fusion.371), kind=kOutput, calls=%fused_computation.63.clone.1 | convolution fusion | flops 320867328 | bytes 20250624 | tf_op jit(solution)/shard_map/while/body/eval_jaxpr/hqk,qhe->khe/dot_general | solution.py:87
  463.2 5.2 fusion.375
  468.3 14.3 %fusion.379 = bf16[3,64,512]{2,1,0:T(8,128)(2,1)S(1)} fusion(bf16[1536,3,64]{0,2,1:T(8,128)(2,1)S(1)} %bitcast.314, f32[3,512,1536]{2,1,0:T(8,128)} %copy-done.3, f32[3,512,1536]{2,1,0:T(8,128)} %fusion.375), kind=kOutput, calls=%fused_computation.92.clone.1 | convolution fusion | flops 320965632 | bytes 19660800 | tf_op jit(solution)/shard_map/while/body/eval_jaxpr/hqk,khe->qhe/dot_general | solution.py:83
  482.7 5.2 fusion.373
  487.8 15.2 %fusion.378 = bf16[3,64,512]{2,1,0:T(8,128)(2,1)} fusion(bf16[1536,3,64]{0,2,1:T(8,128)(2,1)S(1)} %bitcast.315, f32[3,512,1536]{2,1,0:T(8,128)} %copy-done.2, f32[3,512,1536]{2,1,0:T(8,128)} %fusion.373), kind=kOutput, calls=%fused_computation.93.clone.1 | convolution fusion | flops 320965632 | bytes 19660800 | tf_op jit(solution)/shard_map/while/body/eval_jaxpr/hqk,khe->qhe/dot_general | solution.py:83
  503.0 14.3 %fusion.374 = f32[3,64,1536]{2,1,0:T(8,128)} fusion(bf16[512,3,64]{0,2,1:T(8,128)(2,1)S(1)} %bitcast.323, f32[3,512,1536]{2,1,0:T(8,128)} %copy-done.2, f32[3,512,1536]{2,1,0:T(8,128)} %fusion.373), kind=kOutput, calls=%fused_computation.67.clone.1 | convolution fusion | flops 320867328 | bytes 20250624 | tf_op jit(solution)/shard_map/while/body/eval_jaxpr/hqk,qhe->khe/dot_general | solution.py:87
  517.4 13.9 %fusion.376 = bf16[3,64,1536]{2,1,0:T(8,128)(2,1)S(1)} fusion(f32[3,64,1536]{2,1,0:T(8,128)} %fusion.372, f32[3,64,1536]{2,1,0:T(8,128)} %fusion.374, bf16[512,3,64]{0,2,1:T(8,128)(2,1)S(1)} %bitcast.321, f32[3,512,1536]{2,1,0:T(8,128)} %copy-done.3, f32[3,512,1536]{2,1,0:T(8,128)} %fusion.375), kind=kOutput, calls=%fused_computation.79.clone.1 | convolution fusion | flops 321752064 | bytes 22020096 | tf_op jit(solution)/shard_map/while/body/eval_jaxpr/hqk,qhe->khe/dot_general | solution.py:87
  532.9 4.5 fusion.177
  537.5 7.7 bitcast_convert_fusion
  545.3 7.2 fusion.174
  552.7 10.5 convolution_bitcast_fusion
  563.2 9.2 convolution_bitcast_fusion.1
  573.2 8.8 add_convert_fusion.3
  582.4 21.3 %psum.79 = bf16[2,192]{1,0:T(2,128)(2,1)S(1)} all-reduce(bf16[2,192]{1,0:T(2,128)(2,1)S(1)} %slice_reduce_fusion), channel_id=1, replica_groups=mesh['dp'=8,'th'=2,'tw'=2] {'dp'}, use_global_device_ids=true, to_apply=%region_29.30 | all-reduce | flops 384 | bytes 1536 | tf_op jit(solution)/shard_map/psum | solution.py:179
  604.3 4.2 all-reduce.5.cloned.1.call-done
  610.3 47.5 %reduce-scatter.5.cloned.1.call-done = bf16[2,384,768]{2,1,0:T(8,128)(2,1)} async-done(((bf16[2,1536,768]{2,1,0:T(8,128)(2,1)}), bf16[2,384,768]{2,1,0:T(8,128)(2,1)}) %reduce-scatter.5.cloned.1.call-update) | async-done | bytes 1179664 | tf_op jit(solution)/shard_map/reduce_scatter | solution.py:172
  666.0 42.8 %all-reduce = (f32[768]{0:T(1024)}, f32[768]{0:T(1024)}, f32[768]{0:T(1024)}, f32[768]{0:T(1024)}, f32[768]{0:T(1024)}, /*index=5*/f32[3072]{0:T(1024)}, f32[768]{0:T(1024)}) all-reduce(f32[768]{0:T(1024)S(1)} %get-tuple-element.81, f32[768]{0:T(1024)S(1)} %get-tuple-element.85, ...), channel_id=1, replica_groups=mesh['dp'=8,'th'=2,'tw'=2] {'dp','th','tw'}, use_global_device_ids=true, to_apply=%region_24.25 | all-reduce | flops 7680 | bytes 61440 | tf_op jit(solution)/shard_map/psum | solution.py:182
  708.8 61.8 %all-gather.9.cloned.1.call-done = bf16[24,768,192]{1,2,0:T(8,128)(2,1)} async-done(((bf16[3,768,192]{1,2,0:T(8,128)(2,1)}), bf16[24,768,192]{1,2,0:T(8,128)(2,1)}) %all-gather.9.cloned.1.call-update) | async-done | bytes 7077904 | tf_op jit(solution)/shard_map/all_gather | solution.py:8
  770.6 4.2 reduce_sum.255
  776.1 305.1 %all-reduce.7.cloned.1.call-done = (f32[768,3072]{1,0:T(8,128)}, f32[3072,768]{1,0:T(8,128)}) async-done(((f32[768,3072]{1,0:T(8,128)}, f32[3072,768]{1,0:T(8,128)}), (f32[768,3072]{1,0:T(8,128)}, f32[3072,768]{1,0:T(8,128)})) %all-reduce.7.cloned.1.call-update) | async-done | bytes 18874384 | tf_op jit(solution)/shard_map/psum | solution.py:182
  1081.2 8.8 copy.61
  (230 shorter events, 118.3 us)
Async XLA Ops:
  7.2 47.7 %copy-start = (bf16[3,768,192]{1,2,0:T(8,128)(2,1)S(1)}, bf16[3,768,192]{1,2,0:T(8,128)(2,1)}, u32[]{:S(2)}) copy-start(bf16[3,768,192]{1,2,0:T(8,128)(2,1)} %param.23) | copy-start | bytes 2654212
  7.2 7.5 copy-start.47
  7.2 47.7 %all-gather.5.cloned.1.call-start = ((), (), s32[]{:S(2)}) async-start(), calls=%async_computation.2 | async-start | bytes 5898240 | tf_op jit(solution)/shard_map/all_gather | solution.py:120
  14.6 159.3 %reduce-scatter.3.cloned.1.call-start = ((), (), s32[]{:S(2)}) async-start(), calls=%async_computation.3 | async-start | bytes 5898240 | tf_op jit(solution)/shard_map/reduce_scatter | solution.py:127
  14.8 46.8 %copy-start.19 = (s32[2,1536]{1,0:T(2,128)S(1)}, s32[2,1536]{1,0:T(2,128)}, u32[]{:S(2)}) copy-start(s32[2,1536]{1,0:T(2,128)} %param.20) | copy-start | bytes 36868
  120.9 5.0 copy-start.17
  120.9 53.0 %copy-start.5 = (bf16[2,384,768]{2,1,0:T(8,128)(2,1)S(1)}, bf16[2,384,768]{2,1,0:T(8,128)(2,1)}, u32[]{:S(2)}) copy-start(bf16[2,384,768]{2,1,0:T(8,128)(2,1)} %param.19) | copy-start | bytes 3538948
  120.9 53.0 %copy-start.20 = (f32[768]{0:T(1024)S(1)}, f32[768]{0:T(1024)}, u32[]{:S(2)}) copy-start(f32[768]{0:T(1024)} %param.26) | copy-start | bytes 9220
  125.9 51.8 %copy-start.24 = (f32[768]{0:T(1024)S(1)}, f32[768]{0:T(1024)}, u32[]{:S(2)}) copy-start(f32[768]{0:T(1024)} %param.27) | copy-start | bytes 9220
  125.9 51.8 %copy-start.29 = (f32[768]{0:T(1024)S(1)}, f32[768]{0:T(1024)}, u32[]{:S(2)}) copy-start(f32[768]{0:T(1024)} %param.28) | copy-start | bytes 9220
  125.9 51.8 %copy-start.44 = (f32[3072]{0:T(1024)S(1)}, f32[3072]{0:T(1024)}, u32[]{:S(2)}) copy-start(f32[3072]{0:T(1024)} %param.30) | copy-start | bytes 36868
  125.9 147.4 %all-gather.7.cloned.1.call-start = ((), (), s32[]{:S(2)}) async-start(), calls=%async_computation.4 | async-start | bytes 5898240 | tf_op jit(solution)/shard_map/all_gather | solution.py:161
  175.7 57.2 %copy-start.22 = (f32[2,384]{1,0:T(2,128)}, f32[2,384]{1,0:T(2,128)S(1)}, u32[]{:S(2)}) copy-start(f32[2,384]{1,0:T(2,128)S(1)} %broadcast_multiply_fusion) | copy-start | bytes 9220
  177.7 55.3 %copy-start.26 = (f32[2,384]{1,0:T(2,128)}, f32[2,384]{1,0:T(2,128)S(1)}, u32[]{:S(2)}) copy-start(f32[2,384]{1,0:T(2,128)S(1)} %fusion.183) | copy-start | bytes 9220
  186.9 23.4 %copy-start.15 = (bf16[2,384,768]{2,1,0:T(8,128)(2,1)S(1)}, bf16[2,384,768]{2,1,0:T(8,128)(2,1)}, u32[]{:S(2)}) copy-start(bf16[2,384,768]{2,1,0:T(8,128)(2,1)} %param.33) | copy-start | bytes 3538948
  233.0 40.4 %copy-start.28 = (bf16[192,768]{1,0:T(8,128)(2,1)S(1)}, bf16[192,768]{1,0:T(8,128)(2,1)}, u32[]{:S(2)}) copy-start(bf16[192,768]{1,0:T(8,128)(2,1)} %param.25) | copy-start | bytes 884740
  233.0 45.4 %copy-start.38 = (f32[2,384]{1,0:T(2,128)}, f32[2,384]{1,0:T(2,128)S(1)}, u32[]{:S(2)}) copy-start(f32[2,384]{1,0:T(2,128)S(1)} %negate_multiply_fusion.2) | copy-start | bytes 9220
  235.7 372.8 %all-reduce.5.cloned.1.call-start = ((), (), s32[]{:S(2)}) async-start(), calls=%async_computation.6 | async-start | bytes 589824 | tf_op jit(solution)/shard_map/psum | solution.py:180
  281.8 4.9 copy-start.12
  291.8 7.7 copy-start.4
  390.4 14.0 %copy-start.13 = (bf16[3,64,512]{2,1,0:T(8,128)(2,1)S(1)}, bf16[3,64,512]{2,1,0:T(8,128)(2,1)}, u32[]{:S(2)}) copy-start(bf16[3,64,512]{2,1,0:T(8,128)(2,1)} %fusion.377) | copy-start | bytes 589828 | tf_op jit(solution)/shard_map/while
  390.4 14.0 %copy-start.14 = (bf16[3,64,512]{2,1,0:T(8,128)(2,1)S(1)}, bf16[3,64,512]{2,1,0:T(8,128)(2,1)}, u32[]{:S(2)}) copy-start(bf16[3,64,512]{2,1,0:T(8,128)(2,1)} %fusion.378) | copy-start | bytes 589828 | tf_op jit(solution)/shard_map/while
  418.8 7.7 copy-start.4
  517.4 14.0 %copy-start.13 = (bf16[3,64,512]{2,1,0:T(8,128)(2,1)S(1)}, bf16[3,64,512]{2,1,0:T(8,128)(2,1)}, u32[]{:S(2)}) copy-start(bf16[3,64,512]{2,1,0:T(8,128)(2,1)} %fusion.377) | copy-start | bytes 589828 | tf_op jit(solution)/shard_map/while
  517.4 14.0 %copy-start.14 = (bf16[3,64,512]{2,1,0:T(8,128)(2,1)S(1)}, bf16[3,64,512]{2,1,0:T(8,128)(2,1)}, u32[]{:S(2)}) copy-start(bf16[3,64,512]{2,1,0:T(8,128)(2,1)} %fusion.378) | copy-start | bytes 589828 | tf_op jit(solution)/shard_map/while
  537.4 120.4 %reduce-scatter.5.cloned.1.call-start = ((), (), s32[]{:S(2)}) async-start(), calls=%async_computation.5 | async-start | bytes 5898240 | tf_op jit(solution)/shard_map/reduce_scatter | solution.py:172
  545.2 225.4 %all-gather.9.cloned.1.call-start = ((), (), s32[]{:S(2)}) async-start(), calls=%async_computation.7 | async-start | bytes 7962624 | tf_op jit(solution)/shard_map/all_gather | solution.py:8
  552.6 528.7 %all-reduce.7.cloned.1.call-start = ((), (), s32[]{:S(2)}) async-start(), calls=%async_computation.8 | async-start | bytes 37748736 | tf_op jit(solution)/shard_map/psum | solution.py:182
  552.6 10.6 copy-start.6
  552.6 10.6 copy-start.8
  552.6 10.6 copy-start.21
  552.6 10.6 copy-start.23
  552.6 10.6 copy-start.25
  552.7 10.6 copy-start.27
  552.7 10.6 copy-start.30
  573.2 8.8 copy-start.18
  573.2 84.7 %copy-start.32 = (f32[2,384]{1,0:T(2,128)S(1)}, f32[2,384]{1,0:T(2,128)}, u32[]{:S(2)}) copy-start(f32[2,384]{1,0:T(2,128)} %copy-done.31) | copy-start | bytes 9220
  573.2 84.7 %copy-start.33 = (f32[768]{0:T(1024)S(1)}, f32[768]{0:T(1024)}, u32[]{:S(2)}) copy-start(f32[768]{0:T(1024)} %param.21) | copy-start | bytes 9220
  582.0 78.2 %copy-start.41 = (f32[2,384]{1,0:T(2,128)S(1)}, f32[2,384]{1,0:T(2,128)}, u32[]{:S(2)}) copy-start(f32[2,384]{1,0:T(2,128)} %copy-done.40) | copy-start | bytes 9220
  582.0 78.2 %copy-start.37 = (f32[2,384]{1,0:T(2,128)S(1)}, f32[2,384]{1,0:T(2,128)}, u32[]{:S(2)}) copy-start(f32[2,384]{1,0:T(2,128)} %copy-done.36) | copy-start | bytes 9220
  582.0 80.9 %copy-start.35 = (f32[2,384]{1,0:T(2,128)S(1)}, f32[2,384]{1,0:T(2,128)}, u32[]{:S(2)}) copy-start(f32[2,384]{1,0:T(2,128)} %copy-done.34) | copy-start | bytes 9220
  582.0 80.9 %copy-start.39 = (f32[2,384]{1,0:T(2,128)S(1)}, f32[2,384]{1,0:T(2,128)}, u32[]{:S(2)}) copy-start(f32[2,384]{1,0:T(2,128)} %copy-done.38) | copy-start | bytes 9220
  657.9 5.1 copy-start.10
  657.9 5.1 copy-start.11
  657.9 5.1 copy-start.16
  1081.2 8.8 slice-start
  1081.2 8.8 slice-start.1
  1081.2 8.8 slice-start.2
  (18 other events, 56.3 us)
Sparse Core Ops, SparseCore 0:
  14.7 40.1 all-gather.4
  126.0 47.8 reduce-scatter.2
  235.9 37.4 all-gather.6
  537.6 70.9 all-reduce.4
  610.9 46.9 reduce-scatter.4
  660.7 109.8 all-gather.8
  778.7 302.4 all-reduce.6
